TPU v7x, 256 devices: a whole 4x4x8 slice. The times are simulated.
256 devices in a mesh: seq: 32 (over z, y), tp: 8 (over x, core).
Axes of the slice: x: 4, y: 4, z: 8, core: 2. Of those that a mesh axis runs over, the one named last changes fastest.
Arguments:
- query_raw: bfloat16 [16384, 4096], P('seq', 'tp'), may hold values from -6 to 6
- key_raw: bfloat16 [16384, 4096], P('seq', 'tp'), may hold values from -6 to 6
- value_raw: bfloat16 [16384, 4096], P('seq', 'tp'), may hold values from -6 to 6
- conv_taps: float32 [3, 4, 4096], P(None, None, 'tp'), may hold values from -3 to 3
- layout_boxes: int32 [4, 16384], P(None, 'seq'), may hold values from 0 to 1023
- box_tables: bfloat16 [2, 1024, 4096], P(None, None, 'tp'), may hold values from -4 to 4
- log_decay: float32 [32, 16384], P('tp', 'seq'), may hold values from -1 to 0, as said below
- norm_gain: float32 [4096], P('tp'), may hold values from 0.25 to 1.75
- out_weight: bfloat16 [4096, 4096], P('tp', 'seq'), may hold values from -0.09375 to 0.09375
- grad_output: bfloat16 [16384, 4096], P('seq', 'tp'), may hold values from -6 to 6
Outputs:
- layer_out: bfloat16 [16384, 4096], P('seq', 'tp')
- grad_query: bfloat16 [16384, 4096], P('seq', 'tp')
- grad_key: bfloat16 [16384, 4096], P('seq', 'tp')
- grad_value: bfloat16 [16384, 4096], P('seq', 'tp')
- grad_taps: float32 [3, 4, 4096], P(None, None, 'tp')
- grad_tables: float32 [2, 1024, 4096], P(None, None, 'tp')
- grad_gain: float32 [4096], P('tp')
- grad_weight: float32 [4096, 4096], P('tp', 'seq')
Inputs may be any that keep to these rules, and one draw needn't show every extreme that they name: `log_decay`: each entry is the logarithm (at most 0) of one head's state decay at one token.
All inputs are finite; a program needn't handle non-finite values.
Results may differ from a plain program's by a relative error of at most 0.02.
Values may be sent and summed in bfloat16 or wider, within the bound.
A program may use at most 128 MiB of HBM per device.

v0:
```python
import jax
import jax.numpy as jnp
from jax import lax
from jax.sharding import PartitionSpec as P

HIGHEST = lax.Precision.HIGHEST


def shifted(x, axis, by):
    length = lax.axis_size(axis)
    pairs = [(i, i + by) for i in range(length) if 0 <= i + by < length]
    return lax.ppermute(x, axis, pairs)


def entering(x, axis, combine, identity, reverse):
    length, here = (lax.axis_size(axis), lax.axis_index(axis))
    everything = jax.tree.map(
        lambda part, kind: lax.all_gather(part.astype(kind), axis), x, (jnp.bfloat16, jnp.bfloat16)
    )
    start = jax.tree.map(
        lambda part, zero: jnp.broadcast_to(jnp.asarray(zero, part.dtype), part.shape), x, identity
    )

    def turn(k, before):
        at = length - 1 - k if reverse else k
        reached = at > here if reverse else at < here
        new = combine(
            before, jax.tree.map(lambda part, own: part[at].astype(own.dtype), everything, x)
        )
        return jax.tree.map(lambda a, b: jnp.where(reached, a, b), new, before)

    return lax.fori_loop(0, length, turn, start)


def combine(earlier, later):
    return (earlier[0] * later[0], later[0][:, None, None] * earlier[1] + later[1])


def on_device(
    query_raw,
    key_raw,
    value_raw,
    conv_taps,
    layout_boxes,
    box_tables,
    log_decay,
    norm_gain,
    out_weight,
    grad_output,
):
    row_count, feat_width = query_raw.shape
    head_count = log_decay.shape[0]
    head_size = feat_width // head_count
    kernel = conv_taps.shape[1]
    buckets = box_tables.shape[1]
    feature_scale = head_size ** (-0.5)
    stacked = jnp.stack([query_raw, key_raw, value_raw])
    rim_rows = shifted(stacked[:, row_count - (kernel - 1) :, :], "seq", 1)
    padded = jnp.concatenate([rim_rows, stacked], axis=1).astype(jnp.float32)
    conved = jnp.zeros((3, row_count, feat_width), jnp.float32)
    for tap_step in range(kernel):
        conved = (
            conved
            + conv_taps[:, tap_step, None, :]
            * padded[:, kernel - 1 - tap_step : kernel - 1 - tap_step + row_count, :]
        )
    bucket_ids = jnp.arange(buckets, dtype=jnp.int32)

    def count_table(first, second):
        return (first[:, None] == bucket_ids[None, :]).astype(jnp.bfloat16) + (
            second[:, None] == bucket_ids[None, :]
        ).astype(jnp.bfloat16)

    hot_x = count_table(layout_boxes[0], layout_boxes[2])
    hot_y = count_table(layout_boxes[1], layout_boxes[3])
    layout = jnp.dot(hot_x, box_tables[0], preferred_element_type=jnp.float32) + jnp.dot(
        hot_y, box_tables[1], preferred_element_type=jnp.float32
    )
    query_feat = (feature_scale * (conved[0] + layout)).astype(jnp.bfloat16)
    key_feat = (conved[1] + layout).astype(jnp.bfloat16)
    value_feat = conved[2].astype(jnp.bfloat16)

    def split_heads(matrix):
        return matrix.reshape(row_count, head_count, head_size).transpose(1, 0, 2)

    def join_heads(blocks):
        return blocks.transpose(1, 0, 2).reshape(row_count, feat_width)

    query_heads = split_heads(query_feat)
    key_heads = split_heads(key_feat)
    value_heads = split_heads(value_feat)
    decay_sum = jnp.cumsum(log_decay, axis=1)
    decay_total = decay_sum[:, -1]
    head_decay = jnp.exp(decay_sum)[:, :, None]
    tail_decay = jnp.exp(decay_total[:, None] - decay_sum)[:, :, None]
    block_decay = jnp.exp(decay_total)
    positions = jnp.arange(row_count, dtype=jnp.int32)
    causal_mask = positions[:, None] >= positions[None, :]
    decay_mask = jnp.where(
        causal_mask[None],
        jnp.exp(jnp.minimum(decay_sum[:, :, None] - decay_sum[:, None, :], 0.0)),
        0.0,
    )
    identity = (
        jnp.ones((head_count,), jnp.float32),
        jnp.zeros((head_count, head_size, head_size), jnp.float32),
    )
    local_state = jnp.einsum("hsi,hsj->hij", key_heads * tail_decay, value_heads, precision=HIGHEST)
    incoming = entering((block_decay, local_state), "seq", combine, identity, False)[1]
    scores = decay_mask * jnp.einsum(
        "hti,hsi->hts", query_heads, key_heads, preferred_element_type=jnp.float32
    )
    attended = jnp.einsum("hts,hsj->htj", scores, value_heads, precision=HIGHEST)
    attended = attended + head_decay * jnp.einsum(
        "hti,hij->htj", query_heads, incoming, precision=HIGHEST
    )
    inverse = lax.rsqrt(jnp.mean(attended * attended, axis=-1, keepdims=True) + 1e-06)
    unit_norm = attended * inverse
    gain_heads = norm_gain.reshape(head_count, 1, head_size)
    normed = join_heads(unit_norm * gain_heads).astype(jnp.bfloat16)
    partial_sum = jnp.dot(
        normed,
        lax.all_gather(out_weight, "seq", axis=1, tiled=True),
        preferred_element_type=jnp.float32,
    )
    layer_out = lax.psum_scatter(
        partial_sum.astype(jnp.bfloat16), "tp", scatter_dimension=1, tiled=True
    )
    cotangent = lax.all_gather(grad_output, "tp", axis=1, tiled=True)
    contract_last = (((1,), (1,)), ((), ()))
    grad_normed_sum = lax.dot_general(
        cotangent,
        lax.all_gather(out_weight, "seq", axis=1, tiled=True),
        contract_last,
        preferred_element_type=jnp.float32,
    )
    grad_normed = grad_normed_sum.astype(jnp.bfloat16)
    contract_first = (((0,), (0,)), ((), ()))
    weight_terms = lax.dot_general(
        normed, cotangent, contract_first, preferred_element_type=jnp.float32
    )
    grad_weight = lax.psum_scatter(
        weight_terms.astype(jnp.bfloat16), "seq", scatter_dimension=1, tiled=True
    ).astype(jnp.float32)
    grad_heads = split_heads(grad_normed).astype(jnp.float32)
    gain_terms = jnp.sum(grad_heads * unit_norm, axis=1).reshape(feat_width)
    grad_unit = grad_heads * gain_heads
    grad_attended = inverse * (
        grad_unit - unit_norm * jnp.mean(grad_unit * unit_norm, axis=-1, keepdims=True)
    )
    back_state = jnp.einsum(
        "hti,htj->hij", query_heads * head_decay, grad_attended, precision=HIGHEST
    )
    later_state = entering((block_decay, back_state), "seq", combine, identity, True)[1]
    grad_scores = decay_mask * jnp.einsum(
        "htj,hsj->hts", grad_attended, value_heads, precision=HIGHEST
    )
    grad_qh = jnp.einsum(
        "hts,hsi->hti", grad_scores, key_heads, precision=HIGHEST
    ) + head_decay * jnp.einsum("htj,hij->hti", grad_attended, incoming, precision=HIGHEST)
    grad_kh = jnp.einsum(
        "hts,hti->hsi", grad_scores, query_heads, precision=HIGHEST
    ) + tail_decay * jnp.einsum("hsj,hij->hsi", value_heads, later_state, precision=HIGHEST)
    grad_vh = jnp.einsum(
        "hts,htj->hsj", scores, grad_attended, precision=HIGHEST
    ) + tail_decay * jnp.einsum("hsi,hij->hsj", key_heads, later_state, precision=HIGHEST)
    grad_pre = jnp.stack(
        [feature_scale * join_heads(grad_qh), join_heads(grad_kh), join_heads(grad_vh)]
    )
    next_rows = shifted(grad_pre[:, : kernel - 1, :], "seq", -1)
    extended = jnp.concatenate([grad_pre, next_rows], axis=1)
    grad_inputs = jnp.zeros((3, row_count, feat_width), jnp.float32)
    for tap_step in range(kernel):
        grad_inputs = (
            grad_inputs
            + conv_taps[:, tap_step, None, :] * extended[:, tap_step : tap_step + row_count, :]
        )
    tap_terms = jnp.stack(
        [
            jnp.sum(
                grad_pre * padded[:, kernel - 1 - tap_step : kernel - 1 - tap_step + row_count, :],
                axis=1,
            )
            for tap_step in range(kernel)
        ],
        axis=1,
    )
    grad_layout = (grad_pre[0] + grad_pre[1]).astype(jnp.bfloat16)
    table_terms = jnp.stack(
        [
            lax.dot_general(hot_x, grad_layout, contract_first, preferred_element_type=jnp.float32),
            lax.dot_general(hot_y, grad_layout, contract_first, preferred_element_type=jnp.float32),
        ]
    )
    grad_taps, grad_tables, grad_gain = (
        lax.psum(tap_terms.astype(jnp.bfloat16), "seq").astype(jnp.float32),
        lax.psum(table_terms.astype(jnp.bfloat16), "seq").astype(jnp.float32),
        lax.psum(gain_terms.astype(jnp.bfloat16), "seq").astype(jnp.float32),
    )
    grad_query = grad_inputs[0].astype(jnp.bfloat16)
    grad_key = grad_inputs[1].astype(jnp.bfloat16)
    grad_value = grad_inputs[2].astype(jnp.bfloat16)
    return (
        layer_out,
        grad_query,
        grad_key,
        grad_value,
        grad_taps,
        grad_tables,
        grad_gain,
        grad_weight,
    )


def solution(mesh):
    return jax.shard_map(
        on_device,
        mesh=mesh,
        in_specs=(
            P("seq", "tp"),
            P("seq", "tp"),
            P("seq", "tp"),
            P(None, None, "tp"),
            P(None, "seq"),
            P(None, None, "tp"),
            P("tp", "seq"),
            P("tp"),
            P("tp", "seq"),
            P("seq", "tp"),
        ),
        out_specs=(
            P("seq", "tp"),
            P("seq", "tp"),
            P("seq", "tp"),
            P("seq", "tp"),
            P(None, None, "tp"),
            P(None, None, "tp"),
            P("tp"),
            P("tp", "seq"),
        ),
        check_vma=False,
    )
```

profile of v0, /device:TPU:8, one launch (start us, length us, event | category | flops | bytes accessed | tf_op | source)
XLA Modules:
  0.0 769.7 jit_solution(2590251355340707665)
XLA Ops:
  12.7 3.5 collective-permute-start
  18.2 2.3 fusion.59
  20.4 5.0 collective-permute-done
  26.3 3.7 multiply_add_fusion
  31.6 2.0 convolution_convert_fusion.6
  35.2 74.4 %all-reduce = bf16[128]{0:T(256)(128)(2,1)S(1)} all-reduce(bf16[128]{0:T(256)(128)(2,1)S(1)} %dynamic-update-slice), channel_id=2, replica_groups=mesh['seq'=32,'tp'=8] {'seq'}, use_global_device_ids=true, to_apply=%add | all-reduce | flops 128 | bytes 512
  109.8 2.8 fusion.95
  112.6 20.2 %all-gather.8.cloned.1.call-done = bf16[512,4096]{1,0:T(8,128)(2,1)} async-done(((bf16[512,128]{1,0:T(8,128)(2,1)}), bf16[512,4096]{1,0:T(8,128)(2,1)}) %all-gather.8.cloned.1.call-update) | async-done | bytes 4194320 | tf_op jit(solution)/shard_map/all_gather | solution.py:123
  132.8 5.8 convolution_convert_fusion.4
  138.7 78.2 %all-gather.12.cloned.1.call-done = bf16[128,128,128]{2,1,0:T(8,128)(2,1)} async-done(((bf16[4,128,128]{2,1,0:T(8,128)(2,1)}), bf16[128,128,128]{2,1,0:T(8,128)(2,1)}) %all-gather.12.cloned.1.call-update) | async-done | bytes 4194320 | tf_op jit(solution)/shard_map/all_gather | solution.py:18
  216.9 33.9 %while.30 = (s32[]{:T(128)}, f32[4,128,128]{2,1,0:T(8,128)S(1)}, s32[]{:T(128)}, bf16[32,4]{1,0:T(8,128)(2,1)S(1)}, bf16[32,4,128,128]{3,2,1,0:T(8,128)(2,1)}, /*index=5*/s32[]{:T(128)}, s32[]{:T(128)}) while((s32[]{:T(128)}, f32[4,128,128]{2,1,0:T(8,128)S(1)}, s32[]{:T(128)}, bf16[32,4]{1,0:T(8,128)(2,1)S(1)}, ...), condition=%wide.region_3.4_spmd.clone, body=%wide.region_2.3_spmd.clone.sunk | while | flops 327688 | bytes 655513 | solution.py:32
  252.4 6.7 multiply_reduce_fusion.4
  259.6 2.1 convolution_convert_fusion.5
  262.0 1.7 fusion.76
  264.5 6.5 convolution_convert_fusion
  271.0 6.5 copy.96
  277.5 2.0 fusion.108
  279.5 3.9 fusion.39
  283.3 4.5 fusion.36
  287.9 52.6 %all-gather.14.cloned.1.call-done = bf16[128,128,128]{2,1,0:T(8,128)(2,1)} async-done(((bf16[4,128,128]{2,1,0:T(8,128)(2,1)}), bf16[128,128,128]{2,1,0:T(8,128)(2,1)}) %all-gather.14.cloned.1.call-update) | async-done | bytes 4194320 | tf_op jit(solution)/shard_map/all_gather | solution.py:18
  340.5 34.1 %while.31 = (s32[]{:T(128)}, f32[4,128,128]{2,1,0:T(8,128)S(1)}, s32[]{:T(128)}, bf16[32,4]{1,0:T(8,128)(2,1)S(1)}, bf16[32,4,128,128]{3,2,1,0:T(8,128)(2,1)}, /*index=5*/s32[]{:T(128)}, s32[]{:T(128)}, s32[]{:T(128)}, s32[]{:T(128)}) while((s32[]{:T(128)}, f32[4,128,128]{2,1,0:T(8,128)S(1)}, s32[]{:T(128)}, ...), condition=%wide.region_8.9_spmd.clone, body=%wide.region_7.8_spmd.clone.sunk | while | flops 327692 | bytes 655575 | solution.py:32
  374.6 2.0 fusion.48
  381.8 6.6 convolution_convert_fusion.1
  389.6 6.3 fusion.42
  399.3 3.7 collective-permute-start.1
  403.0 2.0 collective-permute-done.1
  408.7 7.6 multiply_reduce_fusion.3
  419.5 136.3 %all-reduce.1 = (bf16[3,4,512]{2,0,1:T(4,128)(2,1)S(1)}, bf16[512]{0:T(512)(128)(2,1)S(1)}) all-reduce(bf16[3,4,512]{2,0,1:T(4,128)(2,1)S(1)} %pad_maximum_fusion.5, bf16[512]{0:T(512)(128)(2,1)S(1)} %bitcast.272), channel_id=1, replica_groups=mesh['seq'=32,'tp'=8] {'seq'}, use_global_device_ids=true, to_apply=%region_13.14 | all-reduce | flops 6656 | bytes 26624 | tf_op jit(solution)/shard_map/psum | solution.py:196
  557.0 7.8 %reduce-scatter.7.cloned.1.call-done = bf16[128,512]{1,0:T(8,128)(2,1)} async-done(((bf16[4096,512]{1,0:T(8,128)(2,1)}), bf16[128,512]{1,0:T(8,128)(2,1)}) %reduce-scatter.7.cloned.1.call-update) | async-done | bytes 131088
  566.5 153.8 %all-reduce.4.cloned.1.call-done = bf16[2,1024,512]{2,1,0:T(8,128)(2,1)} async-done(((bf16[2,1024,512]{2,1,0:T(8,128)(2,1)}), bf16[2,1024,512]{2,1,0:T(8,128)(2,1)}) %all-reduce.4.cloned.1.call-update) | async-done | bytes 2097168 | tf_op jit(solution)/shard_map/psum | solution.py:197
  720.3 4.2 convert_element_type.195
  724.5 38.1 %reduce-scatter.5.cloned.1.call-done = bf16[512,512]{1,0:T(8,128)(2,1)} async-done(((bf16[512,4096]{1,0:T(8,128)(2,1)}), bf16[512,512]{1,0:T(8,128)(2,1)}) %reduce-scatter.5.cloned.1.call-update) | async-done | bytes 524304 | tf_op jit(solution)/shard_map/reduce_scatter | solution.py:126
  (237 shorter events, 99.1 us)
Async XLA Ops:
  7.2 9.0 %copy-start.17 = (f32[4,512]{1,0:T(4,128)S(1)}, f32[4,512]{1,0:T(4,128)}, u32[]{:S(2)}) copy-start(f32[4,512]{1,0:T(4,128)} %param.20) | copy-start | bytes 24580
  7.2 10.8 %copy-start.18 = (s32[4,512]{1,0:T(4,128)S(1)}, s32[4,512]{1,0:T(4,128)}, u32[]{:S(2)}) copy-start(s32[4,512]{1,0:T(4,128)} %param.18) | copy-start | bytes 24580
  7.2 10.9 %copy-start.16 = (f32[3,4,512]{2,1,0:T(4,128)S(1)}, f32[3,4,512]{2,1,0:T(4,128)}, u32[]{:S(2)}) copy-start(f32[3,4,512]{2,1,0:T(4,128)} %param.17) | copy-start | bytes 73732
  7.2 105.4 %all-gather.10.cloned.1.call-start = ((), (), s32[]{:S(2)}) async-start(), calls=%async_computation.4 | async-start | bytes 4718592 | tf_op jit(solution)/shard_map/all_gather | solution.py:129
  7.9 124.9 %all-gather.8.cloned.1.call-start = ((), (), s32[]{:S(2)}) async-start(), calls=%async_computation.2 | async-start | bytes 4325376 | tf_op jit(solution)/shard_map/all_gather | solution.py:123
  8.7 208.2 %all-gather.12.cloned.1.call-start = ((), (), s32[]{:S(2)}) async-start(), calls=%async_computation.6 | async-start | bytes 4325376 | tf_op jit(solution)/shard_map/all_gather | solution.py:18
  12.7 12.7 %collective-permute-start = (bf16[3,3,512]{1,2,0:T(8,128)(2,1)S(1)}, bf16[3,3,512]{1,2,0:T(8,128)(2,1)S(1)}, u32[]{:S(2)}, u32[]{:S(2)}) collective-permute-start(bf16[3,3,512]{1,2,0:T(8,128)(2,1)S(1)} %pad_maximum_fusion.3), channel_id=1, source_target_pairs={{0,8},{8,16},{16,24},{24,32},{32,40},{40,48},{48,56},{56,64},{64,7... | collective-permute-start | bytes 27656 | tf_op jit(solution)/shard_map/ppermute | solution.py:12
  26.3 3.8 copy-start
  26.3 3.9 copy-start.19
  30.1 3.5 copy-start.20
  31.3 81.3 %copy-start.12 = (bf16[512,512]{0,1:T(8,128)(2,1)}, bf16[512,512]{0,1:T(8,128)(2,1)S(1)}, u32[]{:S(2)}) copy-start(bf16[512,512]{0,1:T(8,128)(2,1)S(1)} %get-tuple-element.326) | copy-start | bytes 1572868
  31.6 81.0 %copy-start.6 = (bf16[512,4,128]{2,0,1:T(8,128)(2,1)}, bf16[512,4,128]{2,0,1:T(8,128)(2,1)S(1)}, u32[]{:S(2)}) copy-start(bf16[512,4,128]{2,0,1:T(8,128)(2,1)S(1)} %copy.62) | copy-start | bytes 1572868
  33.6 306.9 %all-gather.14.cloned.1.call-start = ((), (), s32[]{:S(2)}) async-start(), calls=%async_computation.7 | async-start | bytes 4325376 | tf_op jit(solution)/shard_map/all_gather | solution.py:18
  109.8 173.6 %copy-start.14 = (pred[512,512]{1,0:T(8,128)(4,1)}, pred[512,512]{1,0:T(8,128)(4,1)S(1)}, u32[]{:S(2)}) copy-start(pred[512,512]{1,0:T(8,128)(4,1)S(1)} %iota_compare_fusion.4) | copy-start | bytes 786436
  138.7 237.9 %copy-start.5 = (bf16[512,512]{0,1:T(8,128)(2,1)}, bf16[512,512]{0,1:T(8,128)(2,1)S(1)}, u32[]{:S(2)}) copy-start(bf16[512,512]{0,1:T(8,128)(2,1)S(1)} %convolution_convert_fusion.4) | copy-start | bytes 1572868
  251.4 1.1 copy-start.8
  252.4 6.7 copy-start.15
  259.1 18.4 %copy-start.2 = (f32[4,512,128]{1,2,0:T(8,128)}, f32[4,512,128]{1,2,0:T(8,128)S(1)}, u32[]{:S(2)}) copy-start(f32[4,512,128]{1,2,0:T(8,128)S(1)} %get-tuple-element.325) | copy-start | bytes 3145732
  261.7 303.0 %reduce-scatter.7.cloned.1.call-start = ((), (), s32[]{:S(2)}) async-start(), calls=%async_computation.8 | async-start | bytes 4325376
  263.7 0.8 copy-start.9
  279.5 3.9 copy-start.13
  287.8 432.5 %all-reduce.4.cloned.1.call-start = ((), (), s32[]{:S(2)}) async-start(), calls=%async_computation.5 | async-start | bytes 4194304 | tf_op jit(solution)/shard_map/psum | solution.py:197
  374.6 2.0 copy-start.3
  374.6 2.0 copy-start.11
  380.0 1.8 copy-start.10
  381.5 381.1 %reduce-scatter.5.cloned.1.call-start = ((), (), s32[]{:S(2)}) async-start(), calls=%async_computation.3 | async-start | bytes 4718592 | tf_op jit(solution)/shard_map/reduce_scatter | solution.py:126
  388.4 1.2 copy-start.4
  389.6 6.3 copy-start.7
  399.3 5.7 collective-permute-start.1
  406.2 2.4 copy-start.1
Sparse Core Ops, SparseCore 0:
  9.8 37.4 all-gather.9
  49.8 82.9 all-gather.7
  136.0 80.8 all-gather.11
  261.8 78.5 all-gather.13
  344.2 220.4 reduce-scatter.6
  568.1 152.1 all-reduce.3
  723.4 39.1 reduce-scatter.4
where the time goes:
time: 777 us; the launch traced here: 770 us
  waiting for transfers between devices  359 us (46%)
  blocking collectives  211 us (27%)
  other arithmetic  90.9 us (12%)
  matrix products  59 us (8%)
  local copies, waits for them, and re-layouts  24.1 us (3%)
  between operations  15.5 us (2%)
  starting transfers between devices  7.83 us (1%)
    psum x1, waiting for transfers between devices, on_device(): lax.psum(table_terms.astype(jnp.bfloat16), 'seq').astype(jnp.float32)  154 us
    psum x1, blocking collectives, on_device(): lax.psum(tap_terms.astype(jnp.bfloat16), 'seq').astype(jnp.float32)  136 us
    all_gather x2, waiting for transfers between devices, entering(): lax.all_gather(part.astype(kind), axis)  131 us
    unnamed x1, blocking collectives  74.4 us
    select_n x64, other arithmetic, turn(): return jax.tree.map(lambda a, b: jnp.where(reached, a, b), new, before)  64.9 us
    reduce_scatter x1, waiting for transfers between devices, on_device(): lax.psum_scatter(partial_sum.astype(jnp.bfloat16), 'tp', scatter_dimensio...  38.1 us
    all_gather x1, waiting for transfers between devices, on_device(): lax.all_gather(out_weight, 'seq', axis=1, tiled=True)  20.2 us
    unnamed x58, local copies, waits for them, and re-layouts  19.7 us
  transfers between devices with their start and end apart: 9, of which 8 were waited for; matrix products, arithmetic and copies ran while one was open for 17% of the time, Pallas kernels for 0%

commit v1 on v0

--- a/solution.py
+++ b/solution.py
@@ -120,7 +120,9 @@
     normed = join_heads(unit_norm * gain_heads).astype(jnp.bfloat16)
     partial_sum = jnp.dot(
         normed,
-        lax.all_gather(out_weight, "seq", axis=1, tiled=True),
+        jnp.concatenate(
+            lax.all_to_all(jnp.stack([out_weight] * lax.axis_size("seq")), "seq", 0, 0), axis=1
+        ),
         preferred_element_type=jnp.float32,
     )
     layer_out = lax.psum_scatter(

time: 777 us -> 825 us (1.062)
  waiting for transfers between devices: 359 us -> 400 us
    all_gather x2, waiting for transfers between devices: 131 us -> 165 us  [entering(): lax.all_gather(part.astype(kind), axis)]
    unnamed x58 -> x61, local copies, waits for them, and re-layouts: 19.7 us -> 19.7 us
  transfers between devices with their start and end apart: 9 -> 10, of which waited for: 8 -> 8; matrix products, arithmetic and copies ran while one was open for 17% -> 16% of each run, Pallas kernels for 0% -> 0%
where the time goes in v1:
time: 825 us; the launch traced here: 818 us
  waiting for transfers between devices  400 us (48%)
  blocking collectives  210 us (25%)
  other arithmetic  91 us (11%)
  matrix products  59.3 us (7%)
  local copies, waits for them, and re-layouts  26.6 us (3%)
  between operations  15.6 us (2%)
  starting transfers between devices  13.1 us (2%)
    all_gather x2, waiting for transfers between devices, entering(): lax.all_gather(part.astype(kind), axis)  165 us
    psum x1, waiting for transfers between devices, on_device(): lax.psum(table_terms.astype(jnp.bfloat16), 'seq').astype(jnp.float32)  154 us
    psum x1, blocking collectives, on_device(): lax.psum(tap_terms.astype(jnp.bfloat16), 'seq').astype(jnp.float32)  136 us
    unnamed x1, blocking collectives  74.4 us
    select_n x64, other arithmetic, turn(): return jax.tree.map(lambda a, b: jnp.where(reached, a, b), new, before)  64.9 us
    reduce_scatter x1, waiting for transfers between devices, on_device(): lax.psum_scatter(partial_sum.astype(jnp.bfloat16), 'tp', scatter_dimensio...  38.1 us
    all_gather x1, waiting for transfers between devices, on_device(): lax.all_gather(out_weight, 'seq', axis=1, tiled=True)  20.2 us
    unnamed x61, local copies, waits for them, and re-layouts  19.7 us
  transfers between devices with their start and end apart: 10, of which 8 were waited for; matrix products, arithmetic and copies ran while one was open for 16% of the time, Pallas kernels for 0%

profile of v1, /device:TPU:8, one launch (start us, length us, event | category | flops | bytes accessed | tf_op | source)
XLA Modules:
  0.0 818.0 jit_solution(5853545950136247980)
XLA Ops:
  12.7 3.5 collective-permute-start
  18.2 2.3 fusion.59
  20.4 5.0 collective-permute-done
  26.3 3.7 multiply_add_fusion
  31.6 2.0 convolution_convert_fusion.6
  35.2 74.4 %all-reduce = bf16[128]{0:T(256)(128)(2,1)S(1)} all-reduce(bf16[128]{0:T(256)(128)(2,1)S(1)} %dynamic-update-slice), channel_id=2, replica_groups=mesh['seq'=32,'tp'=8] {'seq'}, use_global_device_ids=true, to_apply=%add | all-reduce | flops 128 | bytes 512
  109.8 2.8 fusion.95
  112.6 20.2 %all-gather.10.cloned.1.call-done = bf16[512,4096]{1,0:T(8,128)(2,1)} async-done(((bf16[512,128]{1,0:T(8,128)(2,1)}), bf16[512,4096]{1,0:T(8,128)(2,1)}) %all-gather.10.cloned.1.call-update) | async-done | bytes 4194320 | tf_op jit(solution)/shard_map/all_gather | solution.py:135
  132.8 5.8 convolution_convert_fusion.4
  138.7 78.2 %all-gather.12.cloned.1.call-done = bf16[128,128,128]{2,1,0:T(8,128)(2,1)} async-done(((bf16[4,128,128]{2,1,0:T(8,128)(2,1)}), bf16[128,128,128]{2,1,0:T(8,128)(2,1)}) %all-gather.12.cloned.1.call-update) | async-done | bytes 4194320 | tf_op jit(solution)/shard_map/all_gather | solution.py:18
  216.9 33.9 %while.30 = (s32[]{:T(128)}, f32[4,128,128]{2,1,0:T(8,128)S(1)}, s32[]{:T(128)}, bf16[32,4]{1,0:T(8,128)(2,1)S(1)}, bf16[32,4,128,128]{3,2,1,0:T(8,128)(2,1)}, /*index=5*/s32[]{:T(128)}, s32[]{:T(128)}) while((s32[]{:T(128)}, f32[4,128,128]{2,1,0:T(8,128)S(1)}, s32[]{:T(128)}, bf16[32,4]{1,0:T(8,128)(2,1)S(1)}, ...), condition=%wide.region_3.4_spmd.clone, body=%wide.region_2.3_spmd.clone.sunk | while | flops 327688 | bytes 655513 | solution.py:32
  252.4 6.7 multiply_reduce_fusion.4
  259.6 2.1 convolution_convert_fusion.5
  261.8 2.4 stack.40
  264.3 7.0 all-to-all-start
  274.1 6.5 convolution_convert_fusion
  280.6 6.5 copy.98
  287.1 2.0 fusion.108
  289.1 3.9 fusion.39
  292.9 4.5 fusion.36
  297.5 87.2 %all-gather.14.cloned.1.call-done = bf16[128,128,128]{2,1,0:T(8,128)(2,1)} async-done(((bf16[4,128,128]{2,1,0:T(8,128)(2,1)}), bf16[128,128,128]{2,1,0:T(8,128)(2,1)}) %all-gather.14.cloned.1.call-update) | async-done | bytes 4194320 | tf_op jit(solution)/shard_map/all_gather | solution.py:18
  384.7 34.2 %while.31 = (s32[]{:T(128)}, f32[4,128,128]{2,1,0:T(8,128)S(1)}, s32[]{:T(128)}, bf16[32,4]{1,0:T(8,128)(2,1)S(1)}, bf16[32,4,128,128]{3,2,1,0:T(8,128)(2,1)}, /*index=5*/s32[]{:T(128)}, s32[]{:T(128)}, s32[]{:T(128)}, s32[]{:T(128)}) while((s32[]{:T(128)}, f32[4,128,128]{2,1,0:T(8,128)S(1)}, s32[]{:T(128)}, ...), condition=%wide.region_8.9_spmd.clone, body=%wide.region_7.8_spmd.clone.sunk | while | flops 327692 | bytes 655575 | solution.py:32
  418.9 2.0 fusion.48
  426.1 6.8 convolution_convert_fusion.1
  434.1 6.3 fusion.42
  445.7 3.8 collective-permute-done.1
  453.1 7.6 multiply_reduce_fusion.3
  463.9 135.6 %all-reduce.1 = (bf16[3,4,512]{2,0,1:T(4,128)(2,1)S(1)}, bf16[512]{0:T(512)(128)(2,1)S(1)}) all-reduce(bf16[3,4,512]{2,0,1:T(4,128)(2,1)S(1)} %pad_maximum_fusion.5, bf16[512]{0:T(512)(128)(2,1)S(1)} %bitcast.275), channel_id=1, replica_groups=mesh['seq'=32,'tp'=8] {'seq'}, use_global_device_ids=true, to_apply=%region_13.14 | all-reduce | flops 6656 | bytes 26624 | tf_op jit(solution)/shard_map/psum | solution.py:198
  600.7 12.3 %reduce-scatter.7.cloned.1.call-done = bf16[128,512]{1,0:T(8,128)(2,1)} async-done(((bf16[4096,512]{1,0:T(8,128)(2,1)}), bf16[128,512]{1,0:T(8,128)(2,1)}) %reduce-scatter.7.cloned.1.call-update) | async-done | bytes 131088
  614.7 154.0 %all-reduce.4.cloned.1.call-done = bf16[2,1024,512]{2,1,0:T(8,128)(2,1)} async-done(((bf16[2,1024,512]{2,1,0:T(8,128)(2,1)}), bf16[2,1024,512]{2,1,0:T(8,128)(2,1)}) %all-reduce.4.cloned.1.call-update) | async-done | bytes 2097168 | tf_op jit(solution)/shard_map/psum | solution.py:199
  768.7 4.2 convert_element_type.196
  772.9 38.1 %reduce-scatter.5.cloned.1.call-done = bf16[512,512]{1,0:T(8,128)(2,1)} async-done(((bf16[512,4096]{1,0:T(8,128)(2,1)}), bf16[512,512]{1,0:T(8,128)(2,1)}) %reduce-scatter.5.cloned.1.call-update) | async-done | bytes 524304 | tf_op jit(solution)/shard_map/reduce_scatter | solution.py:128
  (243 shorter events, 102.9 us)
Async XLA Ops:
  7.2 9.0 %copy-start.18 = (f32[4,512]{1,0:T(4,128)S(1)}, f32[4,512]{1,0:T(4,128)}, u32[]{:S(2)}) copy-start(f32[4,512]{1,0:T(4,128)} %param.20) | copy-start | bytes 24580
  7.2 10.8 %copy-start.19 = (s32[4,512]{1,0:T(4,128)S(1)}, s32[4,512]{1,0:T(4,128)}, u32[]{:S(2)}) copy-start(s32[4,512]{1,0:T(4,128)} %param.18) | copy-start | bytes 24580
  7.2 10.9 %copy-start.17 = (f32[3,4,512]{2,1,0:T(4,128)S(1)}, f32[3,4,512]{2,1,0:T(4,128)}, u32[]{:S(2)}) copy-start(f32[3,4,512]{2,1,0:T(4,128)} %param.17) | copy-start | bytes 73732
  7.2 105.4 %all-gather.8.cloned.1.call-start = ((), (), s32[]{:S(2)}) async-start(), calls=%async_computation.4 | async-start | bytes 4718592 | tf_op jit(solution)/shard_map/all_gather | solution.py:131
  7.9 124.9 %all-gather.10.cloned.1.call-start = ((), (), s32[]{:S(2)}) async-start(), calls=%async_computation.5 | async-start | bytes 4325376 | tf_op jit(solution)/shard_map/all_gather | solution.py:135
  8.7 208.2 %all-gather.12.cloned.1.call-start = ((), (), s32[]{:S(2)}) async-start(), calls=%async_computation.7 | async-start | bytes 4325376 | tf_op jit(solution)/shard_map/all_gather | solution.py:18
  12.7 12.7 %collective-permute-start = (bf16[3,3,512]{1,2,0:T(8,128)(2,1)S(1)}, bf16[3,3,512]{1,2,0:T(8,128)(2,1)S(1)}, u32[]{:S(2)}, u32[]{:S(2)}) collective-permute-start(bf16[3,3,512]{1,2,0:T(8,128)(2,1)S(1)} %pad_maximum_fusion.3), channel_id=1, source_target_pairs={{0,8},{8,16},{16,24},{24,32},{32,40},{40,48},{48,56},{56,64},{64,7... | collective-permute-start | bytes 27656 | tf_op jit(solution)/shard_map/ppermute | solution.py:12
  26.3 3.8 copy-start
  26.3 3.9 copy-start.20
  30.1 3.5 copy-start.21
  31.3 81.3 %copy-start.10 = (bf16[512,512]{0,1:T(8,128)(2,1)}, bf16[512,512]{0,1:T(8,128)(2,1)S(1)}, u32[]{:S(2)}) copy-start(bf16[512,512]{0,1:T(8,128)(2,1)S(1)} %get-tuple-element.326) | copy-start | bytes 1572868
  31.6 81.0 %copy-start.6 = (bf16[512,4,128]{2,0,1:T(8,128)(2,1)}, bf16[512,4,128]{2,0,1:T(8,128)(2,1)S(1)}, u32[]{:S(2)}) copy-start(bf16[512,4,128]{2,0,1:T(8,128)(2,1)S(1)} %copy.63) | copy-start | bytes 1572868
  33.6 351.2 %all-gather.14.cloned.1.call-start = ((), (), s32[]{:S(2)}) async-start(), calls=%async_computation.8 | async-start | bytes 4325376 | tf_op jit(solution)/shard_map/all_gather | solution.py:18
  109.8 141.6 %copy-start.14 = (pred[512,512]{1,0:T(8,128)(4,1)}, pred[512,512]{1,0:T(8,128)(4,1)S(1)}, u32[]{:S(2)}) copy-start(pred[512,512]{1,0:T(8,128)(4,1)S(1)} %iota_compare_fusion.4) | copy-start | bytes 786436
  138.7 282.2 %copy-start.5 = (bf16[512,512]{0,1:T(8,128)(2,1)}, bf16[512,512]{0,1:T(8,128)(2,1)S(1)}, u32[]{:S(2)}) copy-start(bf16[512,512]{0,1:T(8,128)(2,1)S(1)} %convolution_convert_fusion.4) | copy-start | bytes 1572868
  251.4 1.0 copy-start.8
  252.4 6.7 copy-start.16
  259.1 28.0 %copy-start.2 = (f32[4,512,128]{1,2,0:T(8,128)}, f32[4,512,128]{1,2,0:T(8,128)S(1)}, u32[]{:S(2)}) copy-start(f32[4,512,128]{1,2,0:T(8,128)S(1)} %get-tuple-element.325) | copy-start | bytes 3145732
  259.1 2.6 copy-start.12
  264.3 161.9 %all-to-all-start = ((bf16[32,512,128]{1,2,0:T(8,128)(2,1)}), bf16[32,512,128]{1,2,0:T(8,128)(2,1)}, u32[]{:S(2)}, u32[]{:S(2)}) async-start(bf16[32,512,128]{1,2,0:T(8,128)(2,1)} %stack.40), calls=%async_computation | async-start | bytes 8388608 | tf_op jit(solution)/shard_map/all_to_all | solution.py:124
  271.3 341.7 %reduce-scatter.7.cloned.1.call-start = ((), (), s32[]{:S(2)}) async-start(), calls=%async_computation.9 | async-start | bytes 4325376
  273.3 0.8 copy-start.13
  287.1 2.0 copy-start.15
  289.1 3.9 copy-start.11
  297.4 471.2 %all-reduce.4.cloned.1.call-start = ((), (), s32[]{:S(2)}) async-start(), calls=%async_computation.6 | async-start | bytes 4194304 | tf_op jit(solution)/shard_map/psum | solution.py:199
  418.9 2.0 copy-start.3
  418.9 2.0 copy-start.9
  425.9 385.1 %reduce-scatter.5.cloned.1.call-start = ((), (), s32[]{:S(2)}) async-start(), calls=%async_computation.3 | async-start | bytes 4718592 | tf_op jit(solution)/shard_map/reduce_scatter | solution.py:128
  432.9 1.2 copy-start.4
  434.1 6.3 copy-start.7
  443.8 5.7 collective-permute-start.1
  450.7 2.4 copy-start.1
Sparse Core Ops, SparseCore 0:
  9.8 37.4 all-gather.7
  49.8 82.9 all-gather.9
  136.0 80.8 all-gather.11
  261.8 122.8 all-gather.13
  388.5 224.4 reduce-scatter.6
  616.3 152.2 all-reduce.3
  771.8 39.1 reduce-scatter.4
